TPU v7x, 32 devices: a whole 2x2x4 slice. The times are simulated.
32 devices in a mesh: section: 2 (over core), expert: 8 (over z, x), head: 2 (over y).
Axes of the slice: x: 2, y: 2, z: 4, core: 2. Of those that a mesh axis runs over, the one named last changes fastest.
Arguments:
- boundary: bfloat16 [2, 2, 1024, 768], P('section', None, 'expert', 'head'), may hold values from -6 to 6
- norm_gain: float32 [2, 768], P('section'), may hold values from 0.25 to 1.75
- gate_prob: float32 [2, 2, 1024], P('section', None, 'expert'), may hold values from 0.25 to 1
- expert_ids: int32 [2, 2, 1024], P('section', None, 'expert'), may hold values from 0 to 7, as said below
- slot_ids: int32 [2, 2, 1024], P('section', None, 'expert'), may hold values from 0 to 32, as said below
- weight_in: bfloat16 [2, 8, 768, 3072], P('section', 'expert', None, 'head'), may hold values from -0.21875 to 0.21875
- weight_out: bfloat16 [2, 8, 3072, 768], P('section', 'expert', 'head'), may hold values from -0.109375 to 0.109375
Outputs:
- boundary_out: bfloat16 [2, 2, 1024, 768], P('section', None, 'expert', 'head')
- grad_in: bfloat16 [2, 8, 768, 3072], P('section', 'expert', None, 'head')
- grad_out: bfloat16 [2, 8, 3072, 768], P('section', 'expert', 'head')
Inputs may be any that keep to these rules, and one draw needn't show every extreme that they name: `expert_ids`: within each layer and micro-batch, tokens are taken in blocks of 128 (the tokens of one index of expert); in every block one expert, the same for all blocks of that layer and micro-batch, is named by more than 32 tokens. `slot_ids`: A token's slot is the number of earlier tokens of its block that name the same expert, capped at 32; 32 means the token is dropped. So at most 32 tokens of a block hold a slot below 32 at one expert, and in every layer and micro-batch one expert has all 32 slots filled from every block.
All inputs are finite; a program needn't handle non-finite values.
Results may differ from a plain program's by a relative error of at most 0.008.
Values may be sent and summed in bfloat16 or wider, within the bound.
A program may use at most 128 MiB of HBM per device.

v0:
```python
import functools

import jax
import jax.numpy as jnp
from jax import lax
from jax.experimental import pallas as pl
from jax.experimental.pallas import tpu as pltpu
from jax.sharding import PartitionSpec as P

EPSILON = 1e-06
ROOT_COEF = 0.7978845608
CUBE_COEF = 0.044715
MESH = pl.DeviceIdType.MESH
BF16 = jnp.bfloat16
F32 = jnp.float32
FWD, BWD = 0, 1
SQUARE, CROSS = 0, 1
COLS = 256
SPLIT = 2
VMEM_LIMIT = 56 * 2**20
COPY_LIMIT = 2**20


def activate(pre_act):
    tangent = jnp.tanh(ROOT_COEF * (pre_act + CUBE_COEF * pre_act * pre_act * pre_act))
    act_value = 0.5 * pre_act * (1.0 + tangent)
    act_slope = 0.5 * (1.0 + tangent) + 0.5 * pre_act * (1.0 - tangent * tangent) * ROOT_COEF * (
        1.0 + 3.0 * CUBE_COEF * pre_act * pre_act
    )
    return (act_value, act_slope)


def dot(left, right, dims=((1,), (0,))):
    return lax.dot_general(left, right, (dims, ((), ())), preferred_element_type=F32)


NT = ((1,), (1,))
TN = ((0,), (0,))


def kernel(
    experts, cap, pad,
    local_ref, gain_ref, prob_ref, ids_ref, slots_ref, win_hbm, wout_hbm,
    out_ref, gin_ref, gout_ref,
    tab, send, rows, normed, act, gpre, mid, keep, away, recvp, back, sec_src, sec_in, xsend, xrecv,
    win_ref, wout_ref, load_sem, turn,
    s1, r1, s2, r2, s3, r3, s4, r4, s5, r5, s6, r6,
):
    win_load = pltpu.make_async_copy(win_hbm, win_ref, load_sem.at[0])
    wout_load = pltpu.make_async_copy(wout_hbm, wout_ref, load_sem.at[1])
    win_load.start()
    wout_load.start()
    sec, me, head = lax.axis_index("section"), lax.axis_index("expert"), lax.axis_index("head")
    other = 1 - head
    micro, tok, half = local_ref.shape
    full = 2 * half
    total = experts * pad
    hidden_half = win_ref.shape[1]
    chunks = hidden_half // COLS
    own_cols = pl.ds(pl.multiple_of(head * half, 128), half)
    other_cols = pl.ds(pl.multiple_of(other * half, 128), half)

    barrier = pltpu.get_barrier_semaphore()

    def each_peer(action):
        def step(k, carry):
            action(lax.rem(me + k, experts))
            return carry

        lax.fori_loop(1, experts, step, 0)

    def greet(d):
        for h in range(2):
            pl.semaphore_signal(
                barrier, inc=1, device_id={"expert": d, "head": h}, device_id_type=MESH
            )

    each_peer(greet)
    pl.semaphore_signal(barrier, inc=1, device_id={"head": other}, device_id_type=MESH)
    pl.semaphore_signal(barrier, inc=1, device_id={"section": 1 - sec}, device_id_type=MESH)

    def slot_rows(index):
        return pl.ds(pl.multiple_of(index * pad, pad), pad)

    def micro_rows(m, index):
        return pl.ds(pl.multiple_of(m * total + index * pad, pad), pad)

    def span(m):
        return slice(m * total, (m + 1) * total)

    eye = lax.broadcasted_iota(jnp.int32, (tok, tok), 0) == lax.broadcasted_iota(
        jnp.int32, (tok, tok), 1
    )

    def to_col(row):
        return jnp.sum(jnp.where(eye, row, 0.0), axis=1, keepdims=True)

    def to_row(col):
        return jnp.sum(jnp.where(eye, col, 0.0), axis=0, keepdims=True)

    for m in range(micro):
        ids, slots = ids_ref[m : m + 1, :], slots_ref[m : m + 1, :]
        target = jnp.where(slots < cap, ids * pad + slots, -1)
        hit = target == lax.broadcasted_iota(jnp.int32, (total, tok), 0)
        tab[m] = jnp.where(hit, 1.0, 0.0).astype(BF16)
    prob = [to_col(prob_ref[m : m + 1, :]) for m in range(micro)]
    gain = gain_ref[...]
    gain_half = gain_ref[:, own_cols]

    def chunk_copy(kind, m, dst, came_from):
        return pltpu.make_async_remote_copy(
            src_ref=send.at[kind, m, slot_rows(dst), :],
            dst_ref=rows.at[kind, micro_rows(m, came_from), own_cols],
            send_sem=s1.at[kind, m, dst],
            recv_sem=r1.at[kind, m, came_from],
            device_id={"expert": dst},
            device_id_type=MESH,
        )

    def cross_copy(kind, m, dst, came_from, cols):
        return pltpu.make_async_remote_copy(
            src_ref=send.at[kind, m, slot_rows(dst), :],
            dst_ref=rows.at[kind, micro_rows(m, came_from), cols],
            send_sem=s2.at[kind, m, dst],
            recv_sem=r2.at[kind, m, came_from],
            device_id={"expert": dst, "head": other},
            device_id_type=MESH,
        )

    def place(kind, m, tokens):
        send[kind, m] = dot(tab[m], tokens).astype(BF16)

    def dispatch(kind, m):
        def both_heads(d):
            cross_copy(kind, m, d, me, own_cols).start()
            chunk_copy(kind, m, d, me).start()

        each_peer(both_heads)
        cross_copy(kind, m, me, me, own_cols).start()
        rows[kind, micro_rows(m, me), own_cols] = send[kind, m, slot_rows(me), :]

    def arrived(kind, m):
        def both_heads(block):
            chunk_copy(kind, m, block, block).wait_recv()
            cross_copy(kind, m, block, block, other_cols).wait_recv()

        cross_copy(kind, m, me, me, other_cols).wait_recv()
        each_peer(both_heads)

    def piece(c):
        return slice(c * (total // SPLIT), (c + 1) * (total // SPLIT))

    def piece_of(m, c):
        return slice(m * total + c * (total // SPLIT), m * total + (c + 1) * (total // SPLIT))

    def away_copy(kind, m, c):
        return pltpu.make_async_remote_copy(
            src_ref=away.at[kind, m, piece(c), :],
            dst_ref=recvp.at[kind, m, piece(c), :],
            send_sem=s3.at[kind, m, c],
            recv_sem=r3.at[kind, m, c],
            device_id={"head": other},
            device_id_type=MESH,
        )

    def back_copy(kind, m, dst, came_from):
        return pltpu.make_async_remote_copy(
            src_ref=keep.at[kind, m, slot_rows(dst), :],
            dst_ref=back.at[kind, m, slot_rows(came_from), :],
            send_sem=s4.at[kind, m, dst],
            recv_sem=r4.at[kind, m, came_from],
            device_id={"expert": dst},
            device_id_type=MESH,
        )

    def send_back(kind, m):
        for c in range(SPLIT):
            away_copy(kind, m, c).wait_recv()
            summed = keep[kind, m, piece(c), :].astype(F32) + recvp[kind, m, piece(c), :].astype(F32)
            keep[kind, m, piece(c), :] = summed.astype(BF16)

            def one(dst, carry):
                @pl.when(dst != me)
                def _():
                    back_copy(kind, m, dst, me).start()

                return carry

            lax.fori_loop(c * experts // SPLIT, (c + 1) * experts // SPLIT, one, 0)
        back[kind, m, slot_rows(me), :] = keep[kind, m, slot_rows(me), :]

    def collect(kind, m):
        each_peer(lambda block: back_copy(kind, m, block, block).wait_recv())
        return dot(tab[m], back[kind, m], TN)

    def section_copy(m):
        return pltpu.make_async_remote_copy(
            src_ref=sec_src.at[m],
            dst_ref=sec_in.at[m],
            send_sem=s5.at[m],
            recv_sem=r5.at[m],
            device_id={"section": 1 - sec},
            device_id_type=MESH,
        )

    def sum_copy(what, m):
        return pltpu.make_async_remote_copy(
            src_ref=xsend.at[what, m],
            dst_ref=xrecv.at[what, m],
            send_sem=s6.at[what, m],
            recv_sem=r6.at[what, m],
            device_id={"head": other},
            device_id_type=MESH,
        )

    def sum_start(what, m, col):
        xsend[what, m] = jnp.broadcast_to(to_row(col), (8, tok))
        sum_copy(what, m).start()

    def sum_done(what, m):
        sum_copy(what, m).wait_recv()
        return to_col(xsend[what, m, 0:1, :] + xrecv[what, m, 0:1, :])

    def square_start(m, tokens):
        values = tokens.astype(F32)
        sum_start(SQUARE, m, jnp.sum(values * values, axis=1, keepdims=True))

    def normalize(m):
        values = rows[FWD, span(m), :].astype(F32)
        inv_scale = lax.rsqrt(jnp.mean(values * values, axis=-1, keepdims=True) + EPSILON)
        normed[span(m), :] = (values * inv_scale * gain).astype(BF16)

    def each_chunk(action):
        def step(c, carry):
            action(pl.ds(pl.multiple_of(c * COLS, COLS), COLS))
            return carry

        lax.fori_loop(0, chunks, step, 0)

    def out_partial(m):
        for c in range(SPLIT):
            away[FWD, m, piece(c), :] = dot(act[piece_of(m, c), :], wout_ref[:, other_cols]).astype(
                BF16
            )
            away_copy(FWD, m, c).start()
        keep[FWD, m] = dot(act[span(m), :], wout_ref[:, own_cols]).astype(BF16)

    def grad_partial(m):
        for c in range(SPLIT):
            away[BWD, m, piece(c), :] = dot(gpre[piece_of(m, c), :], win_ref[other_cols, :], NT).astype(
                BF16
            )
            away_copy(BWD, m, c).start()
        keep[BWD, m] = dot(gpre[span(m), :], win_ref[own_cols, :], NT).astype(BF16)

    def layer_out(m, tokens):
        return (tokens.astype(F32) + prob[m] * collect(FWD, m)).astype(BF16)

    def sent_grad(m, cot):
        return (prob[m] * cot.astype(F32)).astype(BF16)

    def cross_start(m, tokens):
        scaled = gain_half * collect(BWD, m)
        sum_start(CROSS, m, jnp.sum(scaled * tokens.astype(F32), axis=1, keepdims=True))
        return scaled

    def layer_grad(m, tokens, cot, scaled):
        inv = lax.rsqrt(sum_done(SQUARE, m) / full + EPSILON)
        cross = sum_done(CROSS, m)
        values = tokens.astype(F32)
        return (
            cot.astype(F32) + inv * scaled - values * (inv * inv * inv * cross / full)
        ).astype(BF16)

    def weight_grads():
        def first(c, carry):
            part = pl.ds(pl.multiple_of(c * COLS, COLS), COLS)
            gin_ref[part, :] = dot(normed[:, part], gpre[...], TN).astype(BF16)
            return carry

        lax.fori_loop(0, full // COLS, first, 0)

        def second(part):
            gout_ref[part, :] = dot(act[:, part], rows[BWD], TN).astype(BF16)

        each_chunk(second)


    @pl.when(sec == 0)
    def _():
        for m in range(micro):
            place(FWD, m, local_ref[m])
        pl.semaphore_wait(barrier, 2 * experts)
        for m in range(micro):
            dispatch(FWD, m)
        for m in range(micro):
            square_start(m, local_ref[m])
        win_load.wait()
        wout_load.wait()

        def forward(m):
            arrived(FWD, m)
            pl.semaphore_signal(
                turn.at[m], inc=1, device_id={"section": 1 - sec}, device_id_type=MESH
            )
            normalize(m)

            def chunk(part):
                pre = dot(normed[span(m), :], win_ref[:, part])
                value, slope = activate(pre)
                act[span(m), part] = value.astype(BF16)
                mid[span(m), part] = slope.astype(mid.dtype)

            each_chunk(chunk)
            out_partial(m)

        def hidden(m):
            sec_src[m] = layer_out(m, local_ref[m])
            section_copy(m).start()

        forward(0)
        send_back(FWD, 0)
        forward(1)
        hidden(0)
        send_back(FWD, 1)
        hidden(1)

        def grad_in(m):
            section_copy(m).wait_recv()
            place(BWD, m, sent_grad(m, sec_in[m]))
            dispatch(BWD, m)

        def backward(m):
            arrived(BWD, m)

            def chunk(part):
                grad_act = dot(rows[BWD, span(m), :], wout_ref[part, :], NT)
                gpre[span(m), part] = (grad_act * mid[span(m), part].astype(F32)).astype(BF16)

            each_chunk(chunk)
            grad_partial(m)

        grad_in(0)
        backward(0)
        grad_in(1)
        send_back(BWD, 0)
        backward(1)
        scaled0 = cross_start(0, local_ref[0])
        send_back(BWD, 1)
        out_ref[0] = layer_grad(0, local_ref[0], sec_in[0], scaled0)
        weight_grads()
        scaled1 = cross_start(1, local_ref[1])
        out_ref[1] = layer_grad(1, local_ref[1], sec_in[1], scaled1)

    @pl.when(sec != 0)
    def _():
        for m in range(micro):
            place(BWD, m, sent_grad(m, local_ref[m]))
        pl.semaphore_wait(barrier, 2 * experts)
        win_load.wait()
        wout_load.wait()
        for m in range(micro):
            pl.semaphore_wait(turn.at[m], 1)
            dispatch(BWD, m)

        def early_grad(m):
            arrived(BWD, m)

            def early(part):
                grad_act = dot(rows[BWD, span(m), :], wout_ref[part, :], NT)
                mid[span(m), part] = grad_act.astype(mid.dtype)

            each_chunk(early)

        for m in range(micro):
            early_grad(m)

        def hidden_in(m):
            section_copy(m).wait_recv()
            place(FWD, m, sec_in[m])
            dispatch(FWD, m)
            square_start(m, sec_in[m])

        def both(m):
            arrived(FWD, m)
            normalize(m)

            def chunk(part):
                pre = dot(normed[span(m), :], win_ref[:, part])
                value, slope = activate(pre)
                act[span(m), part] = value.astype(BF16)
                gpre[span(m), part] = (mid[span(m), part].astype(F32) * slope).astype(BF16)

            each_chunk(chunk)
            grad_partial(m)

        def finish(m, scaled):
            sec_src[m] = layer_grad(m, sec_in[m], local_ref[m], scaled)
            section_copy(m).start()

        hidden_in(0)
        both(0)
        hidden_in(1)
        send_back(BWD, 0)
        both(1)
        scaled0 = cross_start(0, sec_in[0])
        send_back(BWD, 1)
        finish(0, scaled0)
        out_partial(0)
        scaled1 = cross_start(1, sec_in[1])
        send_back(FWD, 0)
        finish(1, scaled1)
        out_partial(1)
        send_back(FWD, 1)
        weight_grads()
        for m in range(micro):
            out_ref[m] = layer_out(m, sec_in[m])

    for m in range(micro):
        for kind in (FWD, BWD):
            def drain(block):
                chunk_copy(kind, m, block, me).wait_send()
                cross_copy(kind, m, block, me, own_cols).wait_send()
                back_copy(kind, m, block, me).wait_send()

            each_peer(drain)
            cross_copy(kind, m, me, me, own_cols).wait_send()
            for c in range(SPLIT):
                away_copy(kind, m, c).wait_send()
        section_copy(m).wait_send()
        sum_copy(SQUARE, m).wait_send()
        sum_copy(CROSS, m).wait_send()


def copy_out(out_in, gin_in, gout_in, out_ref, gin_ref, gout_ref, sem):
    pairs = ((gin_in, gin_ref), (gout_in, gout_ref), (out_in, out_ref))
    copies = [pltpu.make_async_copy(a, b, sem.at[i]) for i, (a, b) in enumerate(pairs)]
    for copy in copies:
        copy.start()
    for copy in copies:
        copy.wait()


def on_device(boundary, norm_gain, gate_prob, expert_ids, slot_ids, weight_in, weight_out):
    experts = lax.axis_size("expert")
    micro, tok, half = boundary.shape[1:]
    full, hidden_half = weight_in.shape[2:]
    cap = 2 * tok // experts
    pad = -(-cap // 16) * 16
    total = experts * pad
    mid_type = F32 if total <= 512 else BF16
    vmem = pl.BlockSpec(memory_space=pltpu.VMEM)
    anywhere = pl.BlockSpec(memory_space=pl.ANY)
    per_block = pltpu.SemaphoreType.DMA((2, micro, experts))
    per_pair = pltpu.SemaphoreType.DMA((2, micro))
    per_piece = pltpu.SemaphoreType.DMA((2, micro, SPLIT))
    per_micro = pltpu.SemaphoreType.DMA((micro,))
    pieces = pltpu.VMEM((2, micro, total, half), BF16)
    tokens = pltpu.VMEM((micro, tok, half), BF16)
    sums = pltpu.VMEM((2, micro, 8, tok), F32)
    out, grad_in, grad_out = pl.pallas_call(
        functools.partial(kernel, experts, cap, pad),
        out_shape=(
            pltpu.VMEM((micro, tok, half), BF16),
            pltpu.VMEM((full, hidden_half), BF16),
            pltpu.VMEM((hidden_half, full), BF16),
        ),
        in_specs=[vmem] * 5 + [anywhere] * 2,
        out_specs=(vmem, vmem, vmem),
        scratch_shapes=[
            pltpu.VMEM((micro, total, tok), BF16),
            pieces,
            pltpu.VMEM((2, micro * total, full), BF16),
            pltpu.VMEM((micro * total, full), BF16),
            pltpu.VMEM((micro * total, hidden_half), BF16),
            pltpu.VMEM((micro * total, hidden_half), BF16),
            pltpu.VMEM((micro * total, hidden_half), mid_type),
            pieces,
            pieces,
            pieces,
            pieces,
            tokens,
            tokens,
            sums,
            sums,
            pltpu.VMEM((full, hidden_half), BF16),
            pltpu.VMEM((hidden_half, full), BF16),
            pltpu.SemaphoreType.DMA((2,)),
            pltpu.SemaphoreType.REGULAR((micro,)),
            per_block, per_block,
            per_block, per_block,
            per_piece, per_piece,
            per_block, per_block,
            per_micro, per_micro,
            per_pair, per_pair,
        ],
        compiler_params=pltpu.CompilerParams(
            collective_id=0, has_side_effects=True, vmem_limit_bytes=VMEM_LIMIT
        ),
    )(
        boundary[0], norm_gain, gate_prob[0], expert_ids[0], slot_ids[0],
        weight_in[0, 0], weight_out[0, 0],
    )
    results = (out, grad_in, grad_out)
    out, grad_in, grad_out = pl.pallas_call(
        copy_out,
        out_shape=[jax.ShapeDtypeStruct(x.shape, x.dtype) for x in results],
        in_specs=[vmem] * 3,
        out_specs=[anywhere] * 3,
        scratch_shapes=[pltpu.SemaphoreType.DMA((3,))],
        compiler_params=pltpu.CompilerParams(vmem_limit_bytes=COPY_LIMIT),
    )(*results)
    return (out[None], grad_in[None, None], grad_out[None, None])


def solution(mesh):
    placed = (
        P("section", None, "expert", "head"),
        P("section", None),
        P("section", None, "expert"),
        P("section", None, "expert"),
        P("section", None, "expert"),
        P("section", "expert", None, "head"),
        P("section", "expert", "head", None),
    )
    return jax.shard_map(
        on_device,
        mesh=mesh,
        in_specs=placed,
        out_specs=(
            P("section", None, "expert", "head"),
            P("section", "expert", None, "head"),
            P("section", "expert", "head", None),
        ),
        check_vma=False,
    )
```

profile of v0, /device:TPU:0, one launch (start us, length us, event | category | flops | bytes accessed | tf_op | source)
XLA Modules:
  0.0 98.8 jit_solution(5131857220300793160)
XLA Ops:
  0.6 95.8 %shard_map.94 = (bf16[2,128,384]{2,1,0:T(8,128)(2,1)S(1)}, bf16[768,1536]{1,0:T(8,128)(2,1)S(1)}, bf16[1536,768]{1,0:T(8,128)(2,1)S(1)}) custom-call(bf16[2,128,384]{2,1,0:T(8,128)(2,1)} %bitcast.11, f32[1,768]{1,0:T(1,128)} %gain_ref.1, f32[2,128]{1,0:T(2,128)} %bitcast.12, s32[2,128]{1,0:T(2,128)} %bitcast.13, s32[2,128]{1,0:T(2,128)} %bitcast.14, ...), custom_call_target="tpu_custom_call" | custom-call | tf_op jit(solution)/shard_map/pallas_call | solution.py:461
  96.4 2.3 %shard_map.95 = (bf16[2,128,384]{2,1,0:T(8,128)(2,1)}, bf16[768,1536]{1,0:T(8,128)(2,1)}, bf16[1536,768]{1,0:T(8,128)(2,1)}) custom-call(bf16[2,128,384]{2,1,0:T(8,128)(2,1)S(1)} %get-tuple-element.9.out_in, bf16[768,1536]{1,0:T(8,128)(2,1)S(1)} %get-tuple-element.10.gin_in, bf16[1536,768]{1,0:T(8,128)(2,1)S(1)} %get-tuple-element.11.gout_in), custom_call_target="tpu_custom_call" | custom-call | tf_op jit(solution)/shard_map/pallas_call | solution.py:505
where the time goes:
time: 99 us; the launch traced here: 98.8 us
  Pallas kernels  98 us (99%)
    pallas_call x1, Pallas kernels, on_device(): pl.pallas_call(functools.partial(kernel, experts, cap, pad), out_shape=(p...  95.8 us
    pallas_call x1, Pallas kernels, on_device(): pl.pallas_call(copy_out, out_shape=[jax.ShapeDtypeStruct(x.shape, x.dtype...  2.26 us

commit v1 on v0

v1 whole, which is shorter than its diff:
```python
import functools

import jax
import jax.numpy as jnp
from jax import lax
from jax.experimental import pallas as pl
from jax.experimental.pallas import tpu as pltpu
from jax.sharding import PartitionSpec as P

EPSILON = 1e-06
ROOT_COEF = 0.7978845608
CUBE_COEF = 0.044715
MESH = pl.DeviceIdType.MESH
BF16 = jnp.bfloat16
F32 = jnp.float32
FWD, BWD = 0, 1
COLS = 256
SPLIT = 2
VMEM_LIMIT = 56 * 2**20
COPY_LIMIT = 2**20
RELAYED = {"f0": False, "b1": True, "f1": False, "b0": False}


def activate(pre_act):
    tangent = jnp.tanh(ROOT_COEF * (pre_act + CUBE_COEF * pre_act * pre_act * pre_act))
    act_value = 0.5 * pre_act * (1.0 + tangent)
    act_slope = 0.5 * (1.0 + tangent) + 0.5 * pre_act * (1.0 - tangent * tangent) * ROOT_COEF * (
        1.0 + 3.0 * CUBE_COEF * pre_act * pre_act
    )
    return (act_value, act_slope)


def dot(left, right, dims=((1,), (0,))):
    return lax.dot_general(left, right, (dims, ((), ())), preferred_element_type=F32)


NT = ((1,), (1,))
TN = ((0,), (0,))


def kernel(
    experts, cap, pad, relayed,
    local_ref, gain_ref, prob_ref, ids_ref, slots_ref, win_hbm, wout_hbm,
    out_ref, gin_ref, gout_ref,
    tab, tab2, send, rows, normed, act, gpre, mid, inv_ref, keep, away, recvp, back,
    sec_src, sec_in, xsend, xrecv, route, route_in, win_ref, wout_ref, load_sem, turn,
    s1, r1, s2, r2, s3, r3, s4, r4, s5, r5, s6, r6, s7, s8, r8,
):
    win_load = pltpu.make_async_copy(win_hbm, win_ref, load_sem.at[0])
    wout_load = pltpu.make_async_copy(wout_hbm, wout_ref, load_sem.at[1])
    win_load.start()
    wout_load.start()
    sec, me, head = lax.axis_index("section"), lax.axis_index("expert"), lax.axis_index("head")
    other = 1 - head
    upper = lax.div(2 * me, experts)
    micro, tok, half = local_ref.shape
    full = 2 * half
    total = experts * pad
    groups = total // tok
    piece_rows = total // SPLIT
    hidden_half = win_ref.shape[1]
    chunks = hidden_half // COLS
    own_cols = pl.ds(pl.multiple_of(head * half, 128), half)
    other_cols = pl.ds(pl.multiple_of(other * half, 128), half)

    barrier = pltpu.get_barrier_semaphore()

    def greet(k, carry):
        d = lax.rem(me + k, experts)
        for h in range(2):
            pl.semaphore_signal(
                barrier, inc=1, device_id={"expert": d, "head": h}, device_id_type=MESH
            )
        return carry

    lax.fori_loop(1, experts, greet, 0)
    pl.semaphore_signal(barrier, inc=1, device_id={"head": other}, device_id_type=MESH)
    pl.semaphore_signal(barrier, inc=1, device_id={"section": 1 - sec}, device_id_type=MESH)

    def far_first(k):
        return k * upper + (experts - 1 - k) * (1 - upper)

    def near_first(k):
        return far_first(experts - 1 - k)

    def each(order, action, with_me, lo=0, hi=experts):
        def step(k, carry):
            d = order(k)
            if with_me:
                action(d)
            else:
                pl.when(d != me)(lambda: action(d))
            return carry

        lax.fori_loop(lo, hi, step, 0)

    def slot_rows(index):
        return pl.ds(pl.multiple_of(index * pad, pad), pad)

    def micro_rows(m, index):
        return pl.ds(pl.multiple_of(m * total + index * pad, pad), pad)

    def span(m):
        return slice(m * total, (m + 1) * total)

    eye = lax.broadcasted_iota(jnp.int32, (tok, tok), 0) == lax.broadcasted_iota(
        jnp.int32, (tok, tok), 1
    )

    def to_col(row):
        return jnp.sum(jnp.where(eye, row, 0.0), axis=1, keepdims=True)

    def to_row(col):
        return jnp.sum(jnp.where(eye, col, 0.0), axis=0, keepdims=True)

    def fill_tab(ref, m, target):
        place_of = lax.broadcasted_iota(jnp.int32, (total, tok), 0).astype(F32)
        ref[m] = jnp.where(target == place_of, 1.0, 0.0).astype(BF16)

    for m in range(micro):
        ids, slots = ids_ref[m : m + 1, :], slots_ref[m : m + 1, :]
        target = jnp.where(slots < cap, ids * pad + slots, -1).astype(F32)
        fill_tab(tab, m, target)
        route[m : m + 1, :] = target
        route[micro + m : micro + m + 1, :] = prob_ref[m : m + 1, :]
    prob = [to_col(prob_ref[m : m + 1, :]) for m in range(micro)]
    gain = gain_ref[...]

    route_copy = pltpu.make_async_remote_copy(
        src_ref=route,
        dst_ref=route_in,
        send_sem=s8,
        recv_sem=r8,
        device_id={"section": 1 - sec},
        device_id_type=MESH,
    )

    def route_done():
        route_copy.wait_recv()
        for m in range(micro):
            fill_tab(tab2, m, route_in[m : m + 1, :])

    HOME, AWAY = 0, 1

    def target_section(slot):
        return sec if slot == HOME else 1 - sec

    def chunk_copy(slot, kind, m, dst, came_from):
        return pltpu.make_async_remote_copy(
            src_ref=send.at[slot, m, slot_rows(dst), :],
            dst_ref=rows.at[kind, micro_rows(m, came_from), own_cols],
            send_sem=s1.at[slot, m],
            recv_sem=r1.at[kind, m, came_from],
            device_id={"section": target_section(slot), "expert": dst},
            device_id_type=MESH,
        )

    def cross_copy(slot, kind, m, dst, came_from, cols):
        return pltpu.make_async_remote_copy(
            src_ref=send.at[slot, m, slot_rows(dst), :],
            dst_ref=rows.at[kind, micro_rows(m, came_from), cols],
            send_sem=s2.at[slot, m],
            recv_sem=r2.at[kind, m, came_from],
            device_id={"section": target_section(slot), "expert": dst, "head": other},
            device_id_type=MESH,
        )

    def relay_copy(kind, m, block, cols):
        return pltpu.make_async_remote_copy(
            src_ref=rows.at[kind, micro_rows(m, block), cols],
            dst_ref=rows.at[kind, micro_rows(m, block), cols],
            send_sem=s7.at[kind, m],
            recv_sem=r2.at[kind, m, block],
            device_id={"head": other},
            device_id_type=MESH,
        )

    def place(slot, m, tokens):
        table = tab if slot == HOME else tab2
        send[slot, m] = dot(table[m], tokens).astype(BF16)

    def dispatch(slot, kind, m, relay):
        def both_heads(d):
            chunk_copy(slot, kind, m, d, me).start()
            if not relay:
                cross_copy(slot, kind, m, d, me, own_cols).start()

        each(far_first, both_heads, slot == AWAY)
        if slot == HOME:
            rows[kind, micro_rows(m, me), own_cols] = send[slot, m, slot_rows(me), :]
            if not relay:
                cross_copy(slot, kind, m, me, me, own_cols).start()

    def arrived(slot, kind, m, relay):
        def one(block):
            chunk_copy(slot, kind, m, block, block).wait_recv()
            if relay:
                relay_copy(kind, m, block, own_cols).start()

        if slot == HOME and relay:
            relay_copy(kind, m, me, own_cols).start()
        each(near_first, one, slot == AWAY)
        each(
            near_first,
            lambda block: cross_copy(slot, kind, m, block, block, other_cols).wait_recv(),
            True,
        )

    def sent(slot, kind, m, relay):
        blocks = experts if slot == AWAY else experts - 1
        pltpu.make_async_remote_copy(
            src_ref=send.at[slot, m, 0 : blocks * pad, :],
            dst_ref=rows.at[kind, 0 : blocks * pad, own_cols],
            send_sem=s1.at[slot, m],
            recv_sem=r1.at[kind, m, 0],
            device_id={"head": other},
            device_id_type=MESH,
        ).wait_send()
        if not relay:
            pltpu.make_async_remote_copy(
                src_ref=send.at[slot, m],
                dst_ref=rows.at[kind, 0:total, own_cols],
                send_sem=s2.at[slot, m],
                recv_sem=r2.at[kind, m, 0],
                device_id={"head": other},
                device_id_type=MESH,
            ).wait_send()

    def relay_sent(kind, m):
        pltpu.make_async_remote_copy(
            src_ref=rows.at[kind, 0:total, own_cols],
            dst_ref=rows.at[kind, 0:total, own_cols],
            send_sem=s7.at[kind, m],
            recv_sem=r2.at[kind, m, 0],
            device_id={"head": other},
            device_id_type=MESH,
        ).wait_send()

    def piece_at(c):
        p = c * upper + (SPLIT - 1 - c) * (1 - upper)
        return p, pl.ds(pl.multiple_of(p * piece_rows, piece_rows), piece_rows)

    def piece_of(m, c):
        p, _ = piece_at(c)
        return pl.ds(pl.multiple_of(m * total + p * piece_rows, piece_rows), piece_rows)

    def away_copy(kind, m, c):
        _, part = piece_at(c)
        return pltpu.make_async_remote_copy(
            src_ref=away.at[kind, m, part, :],
            dst_ref=recvp.at[kind, m, part, :],
            send_sem=s3.at[kind, m, c],
            recv_sem=r3.at[kind, m, c],
            device_id={"head": other},
            device_id_type=MESH,
        )

    def back_copy(kind, m, dst, came_from):
        return pltpu.make_async_remote_copy(
            src_ref=keep.at[kind, m, slot_rows(dst), :],
            dst_ref=back.at[kind, m, slot_rows(came_from), :],
            send_sem=s4.at[kind, m],
            recv_sem=r4.at[kind, m, came_from],
            device_id={"expert": dst},
            device_id_type=MESH,
        )

    def back_sent(kind, m):
        pltpu.make_async_remote_copy(
            src_ref=keep.at[kind, m, 0 : (experts - 1) * pad, :],
            dst_ref=back.at[kind, m, 0 : (experts - 1) * pad, :],
            send_sem=s4.at[kind, m],
            recv_sem=r4.at[kind, m, 0],
            device_id={"head": other},
            device_id_type=MESH,
        ).wait_send()

    def send_back(kind, m):
        if kind == BWD:
            sum_copy(m).wait_recv()
        for c in range(SPLIT):
            p, part = piece_at(c)
            away_copy(kind, m, c).wait_recv()
            if kind == FWD:
                summed = keep[kind, m, part, :].astype(F32) + recvp[kind, m, part, :].astype(F32)
                keep[kind, m, part, :] = summed.astype(BF16)
            else:
                for i in range(groups // SPLIT):
                    g = p * (groups // SPLIT) + i
                    here = pl.ds(pl.multiple_of(g * tok, tok), tok)
                    there = pl.ds(pl.multiple_of(m * total + g * tok, tok), tok)
                    cross = to_col(xsend[m, pl.ds(g, 1), :] + xrecv[m, pl.ds(g, 1), :])
                    inv = inv_ref[there, :]
                    grad = keep[kind, m, here, :].astype(F32) + recvp[kind, m, here, :].astype(F32)
                    values = rows[FWD, there, own_cols].astype(F32)
                    delta = inv * (gain_ref[:, own_cols] * grad) - values * (
                        inv * inv * inv * cross / full
                    )
                    keep[kind, m, here, :] = delta.astype(BF16)
            each(
                far_first,
                lambda dst: back_copy(kind, m, dst, me).start(),
                False,
                c * experts // SPLIT,
                (c + 1) * experts // SPLIT,
            )
        back[kind, m, slot_rows(me), :] = keep[kind, m, slot_rows(me), :]

    def collect(kind, m):
        each(near_first, lambda block: back_copy(kind, m, block, block).wait_recv(), False)
        return dot(tab[m], back[kind, m], TN)

    def section_copy(m):
        return pltpu.make_async_remote_copy(
            src_ref=sec_src.at[m],
            dst_ref=sec_in.at[m],
            send_sem=s5.at[m],
            recv_sem=r5.at[m],
            device_id={"section": 1 - sec},
            device_id_type=MESH,
        )

    def sum_copy(m):
        return pltpu.make_async_remote_copy(
            src_ref=xsend.at[m],
            dst_ref=xrecv.at[m],
            send_sem=s6.at[m],
            recv_sem=r6.at[m],
            device_id={"head": other},
            device_id_type=MESH,
        )

    def normalize(m):
        values = rows[FWD, span(m), :].astype(F32)
        inv_scale = lax.rsqrt(jnp.mean(values * values, axis=-1, keepdims=True) + EPSILON)
        inv_ref[span(m), :] = inv_scale
        normed[span(m), :] = (values * inv_scale * gain).astype(BF16)

    def each_chunk(action):
        def step(c, carry):
            action(pl.ds(pl.multiple_of(c * COLS, COLS), COLS))
            return carry

        lax.fori_loop(0, chunks, step, 0)

    def out_partial(m):
        for c in range(SPLIT):
            _, part = piece_at(c)
            away[FWD, m, part, :] = dot(act[piece_of(m, c), :], wout_ref[:, other_cols]).astype(
                BF16
            )
            away_copy(FWD, m, c).start()
        keep[FWD, m] = dot(act[span(m), :], wout_ref[:, own_cols]).astype(BF16)

    def grad_partial(m):
        for c in range(SPLIT):
            _, part = piece_at(c)
            away[BWD, m, part, :] = dot(gpre[piece_of(m, c), :], win_ref[other_cols, :], NT).astype(
                BF16
            )
            away_copy(BWD, m, c).start()
        keep[BWD, m] = dot(gpre[span(m), :], win_ref[own_cols, :], NT).astype(BF16)
        for g in range(groups):
            here = slice(g * tok, (g + 1) * tok)
            there = slice(m * total + g * tok, m * total + (g + 1) * tok)
            cross = jnp.zeros((tok, 1), F32)
            for ref, cols in ((away, other_cols), (keep, own_cols)):
                scaled = ref[BWD, m, here, :].astype(F32) * gain_ref[:, cols]
                cross = cross + jnp.sum(
                    scaled * rows[FWD, there, cols].astype(F32), axis=1, keepdims=True
                )
            xsend[m, g : g + 1, :] = to_row(cross)
        sum_copy(m).start()

    def layer_out(m, tokens):
        return (tokens.astype(F32) + prob[m] * collect(FWD, m)).astype(BF16)

    def sent_grad(weight, cot):
        return (weight * cot.astype(F32)).astype(BF16)

    def layer_grad(m, cot):
        return (cot.astype(F32) + collect(BWD, m)).astype(BF16)

    def in_grads():
        def first(c, carry):
            part = pl.ds(pl.multiple_of(c * COLS, COLS), COLS)
            gin_ref[part, :] = dot(normed[:, part], gpre[...], TN).astype(BF16)
            return carry

        lax.fori_loop(0, full // COLS, first, 0)

    def out_grads():
        def second(part):
            gout_ref[part, :] = dot(act[:, part], rows[BWD], TN).astype(BF16)

        each_chunk(second)

    @pl.when(sec == 0)
    def _():
        own_fwd, own_bwd, their_fwd = relayed["f0"], relayed["b0"], relayed["f1"]
        for m in range(micro):
            place(HOME, m, local_ref[m])
        pl.semaphore_wait(barrier, 2 * experts)
        dispatch(HOME, FWD, 0, own_fwd)
        route_copy.start()
        win_load.wait()
        wout_load.wait()

        def forward(m):
            arrived(HOME, FWD, m, own_fwd)
            pl.semaphore_signal(
                turn.at[m], inc=1, device_id={"section": 1 - sec}, device_id_type=MESH
            )
            if m + 1 < micro:
                dispatch(HOME, FWD, m + 1, own_fwd)
            normalize(m)

            def chunk(part):
                pre = dot(normed[span(m), :], win_ref[:, part])
                value, slope = activate(pre)
                act[span(m), part] = value.astype(BF16)
                mid[span(m), part] = slope.astype(mid.dtype)

            each_chunk(chunk)

        def hidden(m):
            sec_src[m] = layer_out(m, local_ref[m])
            place(AWAY, m, sec_src[m])
            dispatch(AWAY, FWD, m, their_fwd)
            section_copy(m).start()

        forward(0)
        out_partial(0)
        route_done()
        forward(1)
        send_back(FWD, 0)
        out_partial(1)
        hidden(0)
        send_back(FWD, 1)
        hidden(1)

        def backward(m):
            arrived(AWAY, BWD, m, own_bwd)

            def chunk(part):
                grad_act = dot(rows[BWD, span(m), :], wout_ref[part, :], NT)
                gpre[span(m), part] = (grad_act * mid[span(m), part].astype(F32)).astype(BF16)

            each_chunk(chunk)

        backward(0)
        grad_partial(0)
        backward(1)
        send_back(BWD, 0)
        grad_partial(1)
        out_grads()
        send_back(BWD, 1)
        section_copy(0).wait_recv()
        out_ref[0] = layer_grad(0, sec_in[0])
        in_grads()
        section_copy(1).wait_recv()
        out_ref[1] = layer_grad(1, sec_in[1])

        for m in range(micro):
            sent(HOME, FWD, m, own_fwd)
            sent(AWAY, FWD, m, their_fwd)
            if own_fwd:
                relay_sent(FWD, m)
            if own_bwd:
                relay_sent(BWD, m)

    @pl.when(sec != 0)
    def _():
        own_bwd, own_fwd, their_bwd = relayed["b1"], relayed["f1"], relayed["b0"]
        for m in range(micro):
            place(HOME, m, sent_grad(prob[m], local_ref[m]))
        pl.semaphore_wait(barrier, 2 * experts)
        route_copy.start()
        win_load.wait()
        wout_load.wait()

        def early_grad(m):
            pl.semaphore_wait(turn.at[m], 1)
            dispatch(HOME, BWD, m, own_bwd)
            arrived(HOME, BWD, m, own_bwd)

            def early(part):
                grad_act = dot(rows[BWD, span(m), :], wout_ref[part, :], NT)
                mid[span(m), part] = grad_act.astype(mid.dtype)

            each_chunk(early)

        early_grad(0)
        route_done()
        prob_in = [to_col(route_in[micro + m : micro + m + 1, :]) for m in range(micro)]
        early_grad(1)

        def both(m):
            arrived(AWAY, FWD, m, own_fwd)
            normalize(m)

            def chunk(part):
                pre = dot(normed[span(m), :], win_ref[:, part])
                value, slope = activate(pre)
                act[span(m), part] = value.astype(BF16)
                gpre[span(m), part] = (mid[span(m), part].astype(F32) * slope).astype(BF16)

            each_chunk(chunk)

        def finish(m):
            sec_src[m] = layer_grad(m, local_ref[m])
            place(AWAY, m, sent_grad(prob_in[m], sec_src[m]))
            dispatch(AWAY, BWD, m, their_bwd)
            section_copy(m).start()

        both(0)
        grad_partial(0)
        both(1)
        send_back(BWD, 0)
        grad_partial(1)
        finish(0)
        send_back(BWD, 1)
        out_partial(0)
        out_partial(1)
        finish(1)
        in_grads()
        out_grads()
        send_back(FWD, 0)
        send_back(FWD, 1)
        for m in range(micro):
            section_copy(m).wait_recv()
            out_ref[m] = layer_out(m, sec_in[m])

        for m in range(micro):
            sent(HOME, BWD, m, own_bwd)
            sent(AWAY, BWD, m, their_bwd)
            if own_fwd:
                relay_sent(FWD, m)
            if own_bwd:
                relay_sent(BWD, m)

    for m in range(micro):
        for kind in (FWD, BWD):
            back_sent(kind, m)
            for c in range(SPLIT):
                away_copy(kind, m, c).wait_send()
        section_copy(m).wait_send()
        sum_copy(m).wait_send()
    route_copy.wait_send()


def copy_out(out_in, gin_in, gout_in, out_ref, gin_ref, gout_ref, sem):
    pairs = ((gin_in, gin_ref), (gout_in, gout_ref), (out_in, out_ref))
    copies = [pltpu.make_async_copy(a, b, sem.at[i]) for i, (a, b) in enumerate(pairs)]
    for copy in copies:
        copy.start()
    for copy in copies:
        copy.wait()


def on_device(boundary, norm_gain, gate_prob, expert_ids, slot_ids, weight_in, weight_out):
    experts = lax.axis_size("expert")
    micro, tok, half = boundary.shape[1:]
    full, hidden_half = weight_in.shape[2:]
    cap = 2 * tok // experts
    pad = -(-cap // 16) * 16
    total = experts * pad
    mid_type = F32 if total <= 512 else BF16
    vmem = pl.BlockSpec(memory_space=pltpu.VMEM)
    anywhere = pl.BlockSpec(memory_space=pl.ANY)
    per_block = pltpu.SemaphoreType.DMA((2, micro, experts))
    per_pair = pltpu.SemaphoreType.DMA((2, micro))
    per_piece = pltpu.SemaphoreType.DMA((2, micro, SPLIT))
    per_micro = pltpu.SemaphoreType.DMA((micro,))
    pieces = pltpu.VMEM((2, micro, total, half), BF16)
    tokens = pltpu.VMEM((micro, tok, half), BF16)
    sums = pltpu.VMEM((micro, max(8, total // tok), tok), F32)
    routes = pltpu.VMEM((8, tok), F32)
    table = pltpu.VMEM((micro, total, tok), BF16)
    out, grad_in, grad_out = pl.pallas_call(
        functools.partial(kernel, experts, cap, pad, RELAYED),
        out_shape=(
            pltpu.VMEM((micro, tok, half), BF16),
            pltpu.VMEM((full, hidden_half), BF16),
            pltpu.VMEM((hidden_half, full), BF16),
        ),
        in_specs=[vmem] * 5 + [anywhere] * 2,
        out_specs=(vmem, vmem, vmem),
        scratch_shapes=[
            table,
            table,
            pieces,
            pltpu.VMEM((2, micro * total, full), BF16),
            pltpu.VMEM((micro * total, full), BF16),
            pltpu.VMEM((micro * total, hidden_half), BF16),
            pltpu.VMEM((micro * total, hidden_half), BF16),
            pltpu.VMEM((micro * total, hidden_half), mid_type),
            pltpu.VMEM((micro * total, 1), F32),
            pieces,
            pieces,
            pieces,
            pieces,
            tokens,
            tokens,
            sums,
            sums,
            routes,
            routes,
            pltpu.VMEM((full, hidden_half), BF16),
            pltpu.VMEM((hidden_half, full), BF16),
            pltpu.SemaphoreType.DMA((2,)),
            pltpu.SemaphoreType.REGULAR((micro,)),
            per_pair, per_block,
            per_pair, per_block,
            per_piece, per_piece,
            per_pair, per_block,
            per_micro, per_micro,
            per_micro, per_micro,
            per_pair,
            pltpu.SemaphoreType.DMA,
            pltpu.SemaphoreType.DMA,
        ],
        compiler_params=pltpu.CompilerParams(
            collective_id=0, has_side_effects=True, vmem_limit_bytes=VMEM_LIMIT
        ),
    )(
        boundary[0], norm_gain, gate_prob[0], expert_ids[0], slot_ids[0],
        weight_in[0, 0], weight_out[0, 0],
    )
    results = (out, grad_in, grad_out)
    out, grad_in, grad_out = pl.pallas_call(
        copy_out,
        out_shape=[jax.ShapeDtypeStruct(x.shape, x.dtype) for x in results],
        in_specs=[vmem] * 3,
        out_specs=[anywhere] * 3,
        scratch_shapes=[pltpu.SemaphoreType.DMA((3,))],
        compiler_params=pltpu.CompilerParams(vmem_limit_bytes=COPY_LIMIT),
    )(*results)
    return (out[None], grad_in[None, None], grad_out[None, None])


def solution(mesh):
    placed = (
        P("section", None, "expert", "head"),
        P("section", None),
        P("section", None, "expert"),
        P("section", None, "expert"),
        P("section", None, "expert"),
        P("section", "expert", None, "head"),
        P("section", "expert", "head", None),
    )
    return jax.shard_map(
        on_device,
        mesh=mesh,
        in_specs=placed,
        out_specs=(
            P("section", None, "expert", "head"),
            P("section", "expert", None, "head"),
            P("section", "expert", "head", None),
        ),
        check_vma=False,
    )
```

time: 99 us -> 91.4 us (0.923)
  Pallas kernels: 98 us -> 90.5 us
    pallas_call x1, Pallas kernels: 95.8 us -> 88.2 us  [on_device(): pl.pallas_call(functools.partial(kernel, experts, cap, pad, RELAYED), out...]
where the time goes in v1:
time: 91.4 us; the launch traced here: 91.3 us
  Pallas kernels  90.5 us (99%)
    pallas_call x1, Pallas kernels, on_device(): pl.pallas_call(functools.partial(kernel, experts, cap, pad, RELAYED), out...  88.2 us
    pallas_call x1, Pallas kernels, on_device(): pl.pallas_call(copy_out, out_shape=[jax.ShapeDtypeStruct(x.shape, x.dtype...  2.26 us

profile of v1, /device:TPU:0, one launch (start us, length us, event | category | flops | bytes accessed | tf_op | source)
XLA Modules:
  0.0 91.3 jit_solution(1863445507551734109)
XLA Ops:
  0.6 88.2 %shard_map.94 = (bf16[2,128,384]{2,1,0:T(8,128)(2,1)S(1)}, bf16[768,1536]{1,0:T(8,128)(2,1)S(1)}, bf16[1536,768]{1,0:T(8,128)(2,1)S(1)}) custom-call(bf16[2,128,384]{2,1,0:T(8,128)(2,1)} %bitcast.11, f32[1,768]{1,0:T(1,128)} %gain_ref.1, f32[2,128]{1,0:T(2,128)} %bitcast.12, s32[2,128]{1,0:T(2,128)} %bitcast.13, s32[2,128]{1,0:T(2,128)} %bitcast.14, ...), custom_call_target="tpu_custom_call" | custom-call | tf_op jit(solution)/shard_map/pallas_call | solution.py:580
  88.9 2.3 %shard_map.95 = (bf16[2,128,384]{2,1,0:T(8,128)(2,1)}, bf16[768,1536]{1,0:T(8,128)(2,1)}, bf16[1536,768]{1,0:T(8,128)(2,1)}) custom-call(bf16[2,128,384]{2,1,0:T(8,128)(2,1)S(1)} %get-tuple-element.9.out_in, bf16[768,1536]{1,0:T(8,128)(2,1)S(1)} %get-tuple-element.10.gin_in, bf16[1536,768]{1,0:T(8,128)(2,1)S(1)} %get-tuple-element.11.gout_in), custom_call_target="tpu_custom_call" | custom-call | tf_op jit(solution)/shard_map/pallas_call | solution.py:631

commit v2 on v1

--- a/solution.py
+++ b/solution.py
@@ -18,7 +18,13 @@
 SPLIT = 2
 VMEM_LIMIT = 56 * 2**20
 COPY_LIMIT = 2**20
-RELAYED = {"f0": False, "b1": True, "f1": False, "b0": False}
+RELAYED = {"f0": (True, True), "b1": (True, True), "f1": (True, False), "b0": (True, False)}
+RELAY_NEAR = True
+TURN_AT = 0
+HOLD = 1
+ORDER = 2
+UNROLL = 6
+PUMP_AT = 0
 
 
 def activate(pre_act):
@@ -185,13 +191,13 @@
             if not relay:
                 cross_copy(slot, kind, m, d, me, own_cols).start()
 
-        each(far_first, both_heads, slot == AWAY)
+        each(near_first if relay and RELAY_NEAR else far_first, both_heads, slot == AWAY)
         if slot == HOME:
             rows[kind, micro_rows(m, me), own_cols] = send[slot, m, slot_rows(me), :]
             if not relay:
                 cross_copy(slot, kind, m, me, me, own_cols).start()
 
-    def arrived(slot, kind, m, relay):
+    def pump(slot, kind, m, relay):
         def one(block):
             chunk_copy(slot, kind, m, block, block).wait_recv()
             if relay:
@@ -200,6 +206,8 @@
         if slot == HOME and relay:
             relay_copy(kind, m, me, own_cols).start()
         each(near_first, one, slot == AWAY)
+
+    def arrived(slot, kind, m):
         each(
             near_first,
             lambda block: cross_copy(slot, kind, m, block, block, other_cols).wait_recv(),
@@ -341,7 +349,7 @@
             action(pl.ds(pl.multiple_of(c * COLS, COLS), COLS))
             return carry
 
-        lax.fori_loop(0, chunks, step, 0)
+        lax.fori_loop(0, chunks, step, 0, unroll=UNROLL if total <= 512 else 1)
 
     def out_partial(m):
         for c in range(SPLIT):
@@ -401,18 +409,28 @@
         for m in range(micro):
             place(HOME, m, local_ref[m])
         pl.semaphore_wait(barrier, 2 * experts)
-        dispatch(HOME, FWD, 0, own_fwd)
+        dispatch(HOME, FWD, 0, own_fwd[0])
+        if own_fwd[1]:
+            dispatch(HOME, FWD, 1, own_fwd[1])
         route_copy.start()
         win_load.wait()
         wout_load.wait()
+        pump(HOME, FWD, 0, own_fwd[0])
+
+        def signal_turn():
+            pl.semaphore_signal(turn, inc=1, device_id={"section": 1 - sec}, device_id_type=MESH)
+
+        if TURN_AT == 0:
+            signal_turn()
+        if PUMP_AT == 0 and own_fwd[1]:
+            pump(HOME, FWD, 1, own_fwd[1])
 
         def forward(m):
-            arrived(HOME, FWD, m, own_fwd)
-            pl.semaphore_signal(
-                turn.at[m], inc=1, device_id={"section": 1 - sec}, device_id_type=MESH
-            )
-            if m + 1 < micro:
-                dispatch(HOME, FWD, m + 1, own_fwd)
+            arrived(HOME, FWD, m)
+            if m == 0 and TURN_AT == 1:
+                signal_turn()
+            if m == 0 and not own_fwd[1]:
+                dispatch(HOME, FWD, 1, own_fwd[1])
             normalize(m)
 
             def chunk(part):
@@ -426,21 +444,28 @@
         def hidden(m):
             sec_src[m] = layer_out(m, local_ref[m])
             place(AWAY, m, sec_src[m])
-            dispatch(AWAY, FWD, m, their_fwd)
+            dispatch(AWAY, FWD, m, their_fwd[m])
             section_copy(m).start()
 
         forward(0)
+        if PUMP_AT == 1 and own_fwd[1]:
+            pump(HOME, FWD, 1, own_fwd[1])
         out_partial(0)
         route_done()
+        if not own_fwd[1]:
+            pump(HOME, FWD, 1, own_fwd[1])
         forward(1)
         send_back(FWD, 0)
+        if HOLD:
+            signal_turn()
         out_partial(1)
         hidden(0)
         send_back(FWD, 1)
         hidden(1)
 
         def backward(m):
-            arrived(AWAY, BWD, m, own_bwd)
+            pump(AWAY, BWD, m, own_bwd[m])
+            arrived(AWAY, BWD, m)
 
             def chunk(part):
                 grad_act = dot(rows[BWD, span(m), :], wout_ref[part, :], NT)
@@ -462,11 +487,11 @@
         out_ref[1] = layer_grad(1, sec_in[1])
 
         for m in range(micro):
-            sent(HOME, FWD, m, own_fwd)
-            sent(AWAY, FWD, m, their_fwd)
-            if own_fwd:
+            sent(HOME, FWD, m, own_fwd[m])
+            sent(AWAY, FWD, m, their_fwd[m])
+            if own_fwd[m]:
                 relay_sent(FWD, m)
-            if own_bwd:
+            if own_bwd[m]:
                 relay_sent(BWD, m)
 
     @pl.when(sec != 0)
@@ -479,10 +504,16 @@
         win_load.wait()
         wout_load.wait()
 
+        pl.semaphore_wait(turn, 1)
+        for m in range(micro):
+            dispatch(HOME, BWD, m, own_bwd[m])
+        if HOLD:
+            pl.semaphore_wait(turn, 1)
+        for m in range(micro):
+            pump(HOME, BWD, m, own_bwd[m])
+
         def early_grad(m):
-            pl.semaphore_wait(turn.at[m], 1)
-            dispatch(HOME, BWD, m, own_bwd)
-            arrived(HOME, BWD, m, own_bwd)
+            arrived(HOME, BWD, m)
 
             def early(part):
                 grad_act = dot(rows[BWD, span(m), :], wout_ref[part, :], NT)
@@ -496,7 +527,7 @@
         early_grad(1)
 
         def both(m):
-            arrived(AWAY, FWD, m, own_fwd)
+            arrived(AWAY, FWD, m)
             normalize(m)
 
             def chunk(part):
@@ -510,15 +541,39 @@
         def finish(m):
             sec_src[m] = layer_grad(m, local_ref[m])
             place(AWAY, m, sent_grad(prob_in[m], sec_src[m]))
-            dispatch(AWAY, BWD, m, their_bwd)
+            dispatch(AWAY, BWD, m, their_bwd[m])
             section_copy(m).start()
 
+        pump(AWAY, FWD, 0, own_fwd[0])
         both(0)
         grad_partial(0)
-        both(1)
-        send_back(BWD, 0)
-        grad_partial(1)
-        finish(0)
+        if ORDER == 0:
+            pump(AWAY, FWD, 1, own_fwd[1])
+            both(1)
+            send_back(BWD, 0)
+            grad_partial(1)
+            finish(0)
+        if ORDER == 1:
+            send_back(BWD, 0)
+            pump(AWAY, FWD, 1, own_fwd[1])
+            both(1)
+            finish(0)
+            grad_partial(1)
+        if ORDER == 2:
+            send_back(BWD, 0)
+            pump(AWAY, FWD, 1, own_fwd[1])
+            both(1)
+            grad_partial(1)
+            finish(0)
+        if ORDER == 3:
+            if own_fwd[1]:
+                pump(AWAY, FWD, 1, own_fwd[1])
+            send_back(BWD, 0)
+            if not own_fwd[1]:
+                pump(AWAY, FWD, 1, own_fwd[1])
+            both(1)
+            finish(0)
+            grad_partial(1)
         send_back(BWD, 1)
         out_partial(0)
         out_partial(1)
@@ -532,11 +587,11 @@
             out_ref[m] = layer_out(m, sec_in[m])
 
         for m in range(micro):
-            sent(HOME, BWD, m, own_bwd)
-            sent(AWAY, BWD, m, their_bwd)
-            if own_fwd:
+            sent(HOME, BWD, m, own_bwd[m])
+            sent(AWAY, BWD, m, their_bwd[m])
+            if own_fwd[m]:
                 relay_sent(FWD, m)
-            if own_bwd:
+            if own_bwd[m]:
                 relay_sent(BWD, m)
 
     for m in range(micro):
@@ -609,7 +664,7 @@
             pltpu.VMEM((full, hidden_half), BF16),
             pltpu.VMEM((hidden_half, full), BF16),
             pltpu.SemaphoreType.DMA((2,)),
-            pltpu.SemaphoreType.REGULAR((micro,)),
+            pltpu.SemaphoreType.REGULAR,
             per_pair, per_block,
             per_pair, per_block,
             per_piece, per_piece,

time: 91.4 us -> 79.2 us (0.87)
  Pallas kernels: 90.5 us -> 78.3 us
    pallas_call x1, Pallas kernels: 88.2 us -> 76 us  [on_device(): pl.pallas_call(functools.partial(kernel, experts, cap, pad, RELAYED), out...]
where the time goes in v2:
time: 79.2 us; the launch traced here: 79.1 us
  Pallas kernels  78.3 us (99%)
  between operations  0.8 us (1%)
    pallas_call x1, Pallas kernels, on_device(): pl.pallas_call(functools.partial(kernel, experts, cap, pad, RELAYED), out...  76 us
    pallas_call x1, Pallas kernels, on_device(): pl.pallas_call(copy_out, out_shape=[jax.ShapeDtypeStruct(x.shape, x.dtype...  2.26 us

profile of v2, /device:TPU:0, one launch (start us, length us, event | category | flops | bytes accessed | tf_op | source)
XLA Modules:
  0.0 79.1 jit_solution(17896623004545617808)
XLA Ops:
  0.6 76.0 %shard_map.94 = (bf16[2,128,384]{2,1,0:T(8,128)(2,1)S(1)}, bf16[768,1536]{1,0:T(8,128)(2,1)S(1)}, bf16[1536,768]{1,0:T(8,128)(2,1)S(1)}) custom-call(bf16[2,128,384]{2,1,0:T(8,128)(2,1)} %bitcast.11, f32[1,768]{1,0:T(1,128)} %gain_ref.1, f32[2,128]{1,0:T(2,128)} %bitcast.12, s32[2,128]{1,0:T(2,128)} %bitcast.13, s32[2,128]{1,0:T(2,128)} %bitcast.14, ...), custom_call_target="tpu_custom_call" | custom-call | tf_op jit(solution)/shard_map/pallas_call | solution.py:635
  76.7 2.3 %shard_map.95 = (bf16[2,128,384]{2,1,0:T(8,128)(2,1)}, bf16[768,1536]{1,0:T(8,128)(2,1)}, bf16[1536,768]{1,0:T(8,128)(2,1)}) custom-call(bf16[2,128,384]{2,1,0:T(8,128)(2,1)S(1)} %get-tuple-element.9.out_in, bf16[768,1536]{1,0:T(8,128)(2,1)S(1)} %get-tuple-element.10.gin_in, bf16[1536,768]{1,0:T(8,128)(2,1)S(1)} %get-tuple-element.11.gout_in), custom_call_target="tpu_custom_call" | custom-call | tf_op jit(solution)/shard_map/pallas_call | solution.py:686

commit v3 on v2

--- a/solution.py
+++ b/solution.py
@@ -19,10 +19,12 @@
 VMEM_LIMIT = 56 * 2**20
 COPY_LIMIT = 2**20
 RELAYED = {"f0": (True, True), "b1": (True, True), "f1": (True, False), "b0": (True, False)}
+DIRECT = {"f0": (True, True), "b1": (True, False), "f1": (False, False), "b0": (False, True)}
 RELAY_NEAR = True
 TURN_AT = 0
 HOLD = 1
-ORDER = 2
+TAIL = 0
+ORDER = 3
 UNROLL = 6
 PUMP_AT = 0
 
@@ -45,17 +47,28 @@
 
 
 def kernel(
-    experts, cap, pad, relayed,
-    local_ref, gain_ref, prob_ref, ids_ref, slots_ref, win_hbm, wout_hbm,
+    experts, cap, pad, relayed, direct,
+    local_hbm, gain_hbm, prob_hbm, ids_hbm, slots_hbm, win_hbm, wout_hbm,
     out_ref, gin_ref, gout_ref,
     tab, tab2, send, rows, normed, act, gpre, mid, inv_ref, keep, away, recvp, back,
-    sec_src, sec_in, xsend, xrecv, route, route_in, win_ref, wout_ref, load_sem, turn,
+    sec_src, sec_in, xsend, xrecv, route, route_in, win_ref, wout_ref,
+    local_ref, gain_ref, prob_ref, ids_ref, slots_ref, load_sem, turn,
     s1, r1, s2, r2, s3, r3, s4, r4, s5, r5, s6, r6, s7, s8, r8,
 ):
+    small = [
+        pltpu.make_async_copy(source, target, load_sem.at[2 + i])
+        for i, (source, target) in enumerate(
+            (
+                (local_hbm, local_ref),
+                (gain_hbm, gain_ref),
+                (prob_hbm, prob_ref),
+                (ids_hbm, ids_ref),
+                (slots_hbm, slots_ref),
+            )
+        )
+    ]
     win_load = pltpu.make_async_copy(win_hbm, win_ref, load_sem.at[0])
     wout_load = pltpu.make_async_copy(wout_hbm, wout_ref, load_sem.at[1])
-    win_load.start()
-    wout_load.start()
     sec, me, head = lax.axis_index("section"), lax.axis_index("expert"), lax.axis_index("head")
     other = 1 - head
     upper = lax.div(2 * me, experts)
@@ -82,6 +95,12 @@
     lax.fori_loop(1, experts, greet, 0)
     pl.semaphore_signal(barrier, inc=1, device_id={"head": other}, device_id_type=MESH)
     pl.semaphore_signal(barrier, inc=1, device_id={"section": 1 - sec}, device_id_type=MESH)
+    for load in small:
+        load.start()
+    win_load.start()
+    wout_load.start()
+    for load in small:
+        load.wait()
 
     def far_first(k):
         return k * upper + (experts - 1 - k) * (1 - upper)
@@ -166,7 +185,7 @@
             src_ref=send.at[slot, m, slot_rows(dst), :],
             dst_ref=rows.at[kind, micro_rows(m, came_from), cols],
             send_sem=s2.at[slot, m],
-            recv_sem=r2.at[kind, m, came_from],
+            recv_sem=r2.at[kind, m],
             device_id={"section": target_section(slot), "expert": dst, "head": other},
             device_id_type=MESH,
         )
@@ -176,7 +195,7 @@
             src_ref=rows.at[kind, micro_rows(m, block), cols],
             dst_ref=rows.at[kind, micro_rows(m, block), cols],
             send_sem=s7.at[kind, m],
-            recv_sem=r2.at[kind, m, block],
+            recv_sem=r2.at[kind, m],
             device_id={"head": other},
             device_id_type=MESH,
         )
@@ -207,12 +226,8 @@
             relay_copy(kind, m, me, own_cols).start()
         each(near_first, one, slot == AWAY)
 
-    def arrived(slot, kind, m):
-        each(
-            near_first,
-            lambda block: cross_copy(slot, kind, m, block, block, other_cols).wait_recv(),
-            True,
-        )
+    def arrived(kind, m):
+        relayed_blocks(kind, m, other_cols).wait_recv()
 
     def sent(slot, kind, m, relay):
         blocks = experts if slot == AWAY else experts - 1
@@ -229,28 +244,27 @@
                 src_ref=send.at[slot, m],
                 dst_ref=rows.at[kind, 0:total, own_cols],
                 send_sem=s2.at[slot, m],
-                recv_sem=r2.at[kind, m, 0],
+                recv_sem=r2.at[kind, m],
                 device_id={"head": other},
                 device_id_type=MESH,
             ).wait_send()
 
+    def relayed_blocks(kind, m, cols):
+        return pltpu.make_async_remote_copy(
+            src_ref=rows.at[kind, span(m), cols],
+            dst_ref=rows.at[kind, span(m), cols],
+            send_sem=s7.at[kind, m],
+            recv_sem=r2.at[kind, m],
+            device_id={"head": other},
+            device_id_type=MESH,
+        )
+
     def relay_sent(kind, m):
-        pltpu.make_async_remote_copy(
-            src_ref=rows.at[kind, 0:total, own_cols],
-            dst_ref=rows.at[kind, 0:total, own_cols],
-            send_sem=s7.at[kind, m],
-            recv_sem=r2.at[kind, m, 0],
-            device_id={"head": other},
-            device_id_type=MESH,
-        ).wait_send()
+        relayed_blocks(kind, m, own_cols).wait_send()
 
     def piece_at(c):
         p = c * upper + (SPLIT - 1 - c) * (1 - upper)
         return p, pl.ds(pl.multiple_of(p * piece_rows, piece_rows), piece_rows)
-
-    def piece_of(m, c):
-        p, _ = piece_at(c)
-        return pl.ds(pl.multiple_of(m * total + p * piece_rows, piece_rows), piece_rows)
 
     def away_copy(kind, m, c):
         _, part = piece_at(c)
@@ -268,20 +282,52 @@
             src_ref=keep.at[kind, m, slot_rows(dst), :],
             dst_ref=back.at[kind, m, slot_rows(came_from), :],
             send_sem=s4.at[kind, m],
-            recv_sem=r4.at[kind, m, came_from],
+            recv_sem=r4.at[kind, m],
             device_id={"expert": dst},
             device_id_type=MESH,
         )
 
-    def back_sent(kind, m):
-        pltpu.make_async_remote_copy(
+    def straight_copy(kind, m, dst, came_from):
+        return pltpu.make_async_remote_copy(
+            src_ref=away.at[kind, m, slot_rows(dst), :],
+            dst_ref=recvp.at[kind, m, slot_rows(came_from), :],
+            send_sem=s3.at[kind, m, 0],
+            recv_sem=r3.at[kind, m, 0],
+            device_id={"expert": dst, "head": other},
+            device_id_type=MESH,
+        )
+
+    def straight_blocks(kind, m):
+        return pltpu.make_async_remote_copy(
+            src_ref=away.at[kind, m],
+            dst_ref=recvp.at[kind, m],
+            send_sem=s3.at[kind, m, 0],
+            recv_sem=r3.at[kind, m, 0],
+            device_id={"head": other},
+            device_id_type=MESH,
+        )
+
+    def piece_blocks(c):
+        return c * experts // SPLIT, (c + 1) * experts // SPLIT
+
+    def send_straight(kind, m, lo, hi):
+        each(far_first, lambda dst: straight_copy(kind, m, dst, me).start(), True, lo, hi)
+
+    def send_same(kind, m, lo, hi):
+        each(far_first, lambda dst: back_copy(kind, m, dst, me).start(), False, lo, hi)
+
+    def keep_own(kind, m):
+        back[kind, m, slot_rows(me), :] = keep[kind, m, slot_rows(me), :]
+
+    def back_blocks(kind, m):
+        return pltpu.make_async_remote_copy(
             src_ref=keep.at[kind, m, 0 : (experts - 1) * pad, :],
             dst_ref=back.at[kind, m, 0 : (experts - 1) * pad, :],
             send_sem=s4.at[kind, m],
-            recv_sem=r4.at[kind, m, 0],
+            recv_sem=r4.at[kind, m],
             device_id={"head": other},
             device_id_type=MESH,
-        ).wait_send()
+        )
 
     def send_back(kind, m):
         if kind == BWD:
@@ -305,18 +351,16 @@
                         inv * inv * inv * cross / full
                     )
                     keep[kind, m, here, :] = delta.astype(BF16)
-            each(
-                far_first,
-                lambda dst: back_copy(kind, m, dst, me).start(),
-                False,
-                c * experts // SPLIT,
-                (c + 1) * experts // SPLIT,
-            )
-        back[kind, m, slot_rows(me), :] = keep[kind, m, slot_rows(me), :]
-
-    def collect(kind, m):
-        each(near_first, lambda block: back_copy(kind, m, block, block).wait_recv(), False)
-        return dot(tab[m], back[kind, m], TN)
+            send_same(kind, m, *piece_blocks(c))
+        keep_own(kind, m)
+
+    def collect(kind, m, straight):
+        back_blocks(kind, m).wait_recv()
+        found = dot(tab[m], back[kind, m], TN)
+        if straight:
+            straight_blocks(kind, m).wait_recv()
+            found = found + dot(tab[m], recvp[kind, m], TN)
+        return found
 
     def section_copy(m):
         return pltpu.make_async_remote_copy(
@@ -351,21 +395,47 @@
 
         lax.fori_loop(0, chunks, step, 0, unroll=UNROLL if total <= 512 else 1)
 
-    def out_partial(m):
+    def out_partial(m, straight):
+        away[FWD, m] = dot(act[span(m), :], wout_ref[:, other_cols]).astype(BF16)
+        if straight:
+            send_straight(FWD, m, 0, experts)
+        else:
+            for c in range(SPLIT):
+                away_copy(FWD, m, c).start()
+        keep[FWD, m] = dot(act[span(m), :], wout_ref[:, own_cols]).astype(BF16)
+        if straight:
+            send_same(FWD, m, 0, experts)
+            keep_own(FWD, m)
+
+    def grad_straight(m):
+        away[BWD, m] = dot(gpre[span(m), :], win_ref[other_cols, :], NT).astype(BF16)
+        keep[BWD, m] = dot(gpre[span(m), :], win_ref[own_cols, :], NT).astype(BF16)
+        sides = ((away, other_cols), (keep, own_cols))
         for c in range(SPLIT):
-            _, part = piece_at(c)
-            away[FWD, m, part, :] = dot(act[piece_of(m, c), :], wout_ref[:, other_cols]).astype(
-                BF16
-            )
-            away_copy(FWD, m, c).start()
-        keep[FWD, m] = dot(act[span(m), :], wout_ref[:, own_cols]).astype(BF16)
-
-    def grad_partial(m):
+            p, _ = piece_at(c)
+            for i in range(groups // SPLIT):
+                g = p * (groups // SPLIT) + i
+                here = pl.ds(pl.multiple_of(g * tok, tok), tok)
+                there = pl.ds(pl.multiple_of(m * total + g * tok, tok), tok)
+                scaled = [ref[BWD, m, here, :].astype(F32) * gain_ref[:, cols] for ref, cols in sides]
+                values = [rows[FWD, there, cols].astype(F32) for _, cols in sides]
+                cross = jnp.sum(
+                    scaled[0] * values[0] + scaled[1] * values[1], axis=1, keepdims=True
+                )
+                inv = inv_ref[there, :]
+                cubed = inv * inv * inv * cross / full
+                for (ref, _), part, value in zip(sides, scaled, values):
+                    ref[BWD, m, here, :] = (inv * part - value * cubed).astype(BF16)
+            send_straight(BWD, m, *piece_blocks(c))
+            send_same(BWD, m, *piece_blocks(c))
+        keep_own(BWD, m)
+
+    def grad_partial(m, straight):
+        if straight:
+            grad_straight(m)
+            return
+        away[BWD, m] = dot(gpre[span(m), :], win_ref[other_cols, :], NT).astype(BF16)
         for c in range(SPLIT):
-            _, part = piece_at(c)
-            away[BWD, m, part, :] = dot(gpre[piece_of(m, c), :], win_ref[other_cols, :], NT).astype(
-                BF16
-            )
             away_copy(BWD, m, c).start()
         keep[BWD, m] = dot(gpre[span(m), :], win_ref[own_cols, :], NT).astype(BF16)
         for g in range(groups):
@@ -380,14 +450,24 @@
             xsend[m, g : g + 1, :] = to_row(cross)
         sum_copy(m).start()
 
-    def layer_out(m, tokens):
-        return (tokens.astype(F32) + prob[m] * collect(FWD, m)).astype(BF16)
+    def layer_out(m, tokens, straight):
+        return (tokens.astype(F32) + prob[m] * collect(FWD, m, straight)).astype(BF16)
 
     def sent_grad(weight, cot):
         return (weight * cot.astype(F32)).astype(BF16)
 
-    def layer_grad(m, cot):
-        return (cot.astype(F32) + collect(BWD, m)).astype(BF16)
+    def layer_grad(m, cot, straight):
+        return (cot.astype(F32) + collect(BWD, m, straight)).astype(BF16)
+
+    def left(kind, m, straight):
+        back_blocks(kind, m).wait_send()
+        if straight:
+            straight_blocks(kind, m).wait_send()
+            return
+        for c in range(SPLIT):
+            away_copy(kind, m, c).wait_send()
+        if kind == BWD:
+            sum_copy(m).wait_send()
 
     def in_grads():
         def first(c, carry):
@@ -395,7 +475,7 @@
             gin_ref[part, :] = dot(normed[:, part], gpre[...], TN).astype(BF16)
             return carry
 
-        lax.fori_loop(0, full // COLS, first, 0)
+        lax.fori_loop(0, full // COLS, first, 0, unroll=3 if total <= 512 else 1)
 
     def out_grads():
         def second(part):
@@ -406,6 +486,7 @@
     @pl.when(sec == 0)
     def _():
         own_fwd, own_bwd, their_fwd = relayed["f0"], relayed["b0"], relayed["f1"]
+        fwd_straight, bwd_straight = direct["f0"], direct["b0"]
         for m in range(micro):
             place(HOME, m, local_ref[m])
         pl.semaphore_wait(barrier, 2 * experts)
@@ -426,7 +507,7 @@
             pump(HOME, FWD, 1, own_fwd[1])
 
         def forward(m):
-            arrived(HOME, FWD, m)
+            arrived(FWD, m)
             if m == 0 and TURN_AT == 1:
                 signal_turn()
             if m == 0 and not own_fwd[1]:
@@ -442,7 +523,7 @@
             each_chunk(chunk)
 
         def hidden(m):
-            sec_src[m] = layer_out(m, local_ref[m])
+            sec_src[m] = layer_out(m, local_ref[m], fwd_straight[m])
             place(AWAY, m, sec_src[m])
             dispatch(AWAY, FWD, m, their_fwd[m])
             section_copy(m).start()
@@ -450,22 +531,26 @@
         forward(0)
         if PUMP_AT == 1 and own_fwd[1]:
             pump(HOME, FWD, 1, own_fwd[1])
-        out_partial(0)
+        out_partial(0, fwd_straight[0])
         route_done()
         if not own_fwd[1]:
             pump(HOME, FWD, 1, own_fwd[1])
         forward(1)
-        send_back(FWD, 0)
-        if HOLD:
+        if not fwd_straight[0]:
+            send_back(FWD, 0)
+        if HOLD == 1:
             signal_turn()
-        out_partial(1)
+        out_partial(1, fwd_straight[1])
         hidden(0)
-        send_back(FWD, 1)
+        if HOLD == 2:
+            signal_turn()
+        if not fwd_straight[1]:
+            send_back(FWD, 1)
         hidden(1)
 
         def backward(m):
             pump(AWAY, BWD, m, own_bwd[m])
-            arrived(AWAY, BWD, m)
+            arrived(BWD, m)
 
             def chunk(part):
                 grad_act = dot(rows[BWD, span(m), :], wout_ref[part, :], NT)
@@ -474,19 +559,23 @@
             each_chunk(chunk)
 
         backward(0)
-        grad_partial(0)
+        grad_partial(0, bwd_straight[0])
         backward(1)
-        send_back(BWD, 0)
-        grad_partial(1)
+        if not bwd_straight[0]:
+            send_back(BWD, 0)
+        grad_partial(1, bwd_straight[1])
         out_grads()
-        send_back(BWD, 1)
+        if not bwd_straight[1]:
+            send_back(BWD, 1)
         section_copy(0).wait_recv()
-        out_ref[0] = layer_grad(0, sec_in[0])
+        out_ref[0] = layer_grad(0, sec_in[0], bwd_straight[0])
         in_grads()
         section_copy(1).wait_recv()
-        out_ref[1] = layer_grad(1, sec_in[1])
+        out_ref[1] = layer_grad(1, sec_in[1], bwd_straight[1])
 
         for m in range(micro):
+            left(FWD, m, fwd_straight[m])
+            left(BWD, m, bwd_straight[m])
             sent(HOME, FWD, m, own_fwd[m])
             sent(AWAY, FWD, m, their_fwd[m])
             if own_fwd[m]:
@@ -497,6 +586,7 @@
     @pl.when(sec != 0)
     def _():
         own_bwd, own_fwd, their_bwd = relayed["b1"], relayed["f1"], relayed["b0"]
+        fwd_straight, bwd_straight = direct["f1"], direct["b1"]
         for m in range(micro):
             place(HOME, m, sent_grad(prob[m], local_ref[m]))
         pl.semaphore_wait(barrier, 2 * experts)
@@ -513,7 +603,7 @@
             pump(HOME, BWD, m, own_bwd[m])
 
         def early_grad(m):
-            arrived(HOME, BWD, m)
+            arrived(BWD, m)
 
             def early(part):
                 grad_act = dot(rows[BWD, span(m), :], wout_ref[part, :], NT)
@@ -527,7 +617,7 @@
         early_grad(1)
 
         def both(m):
-            arrived(AWAY, FWD, m)
+            arrived(FWD, m)
             normalize(m)
 
             def chunk(part):
@@ -539,54 +629,53 @@
             each_chunk(chunk)
 
         def finish(m):
-            sec_src[m] = layer_grad(m, local_ref[m])
+            sec_src[m] = layer_grad(m, local_ref[m], bwd_straight[m])
             place(AWAY, m, sent_grad(prob_in[m], sec_src[m]))
             dispatch(AWAY, BWD, m, their_bwd[m])
             section_copy(m).start()
 
         pump(AWAY, FWD, 0, own_fwd[0])
         both(0)
-        grad_partial(0)
-        if ORDER == 0:
-            pump(AWAY, FWD, 1, own_fwd[1])
-            both(1)
+        grad_partial(0, bwd_straight[0])
+        if not bwd_straight[0]:
             send_back(BWD, 0)
-            grad_partial(1)
+        if ORDER == 1:
             finish(0)
-        if ORDER == 1:
-            send_back(BWD, 0)
-            pump(AWAY, FWD, 1, own_fwd[1])
-            both(1)
+        pump(AWAY, FWD, 1, own_fwd[1])
+        both(1)
+        if ORDER == 2:
             finish(0)
-            grad_partial(1)
-        if ORDER == 2:
-            send_back(BWD, 0)
-            pump(AWAY, FWD, 1, own_fwd[1])
-            both(1)
-            grad_partial(1)
+        grad_partial(1, bwd_straight[1])
+        if ORDER == 3:
             finish(0)
-        if ORDER == 3:
-            if own_fwd[1]:
-                pump(AWAY, FWD, 1, own_fwd[1])
-            send_back(BWD, 0)
-            if not own_fwd[1]:
-                pump(AWAY, FWD, 1, own_fwd[1])
-            both(1)
-            finish(0)
-            grad_partial(1)
-        send_back(BWD, 1)
-        out_partial(0)
-        out_partial(1)
+        if not bwd_straight[1]:
+            send_back(BWD, 1)
+        if TAIL == 0:
+            out_partial(0, fwd_straight[0])
+            out_partial(1, fwd_straight[1])
         finish(1)
+        if TAIL == 1:
+            out_partial(0, fwd_straight[0])
+            out_partial(1, fwd_straight[1])
         in_grads()
+        if TAIL == 2:
+            out_partial(0, fwd_straight[0])
+            out_partial(1, fwd_straight[1])
         out_grads()
-        send_back(FWD, 0)
-        send_back(FWD, 1)
+        if TAIL == 3:
+            out_partial(0, fwd_straight[0])
+            out_partial(1, fwd_straight[1])
+        if not fwd_straight[0]:
+            send_back(FWD, 0)
+        if not fwd_straight[1]:
+            send_back(FWD, 1)
         for m in range(micro):
             section_copy(m).wait_recv()
-            out_ref[m] = layer_out(m, sec_in[m])
+            out_ref[m] = layer_out(m, sec_in[m], fwd_straight[m])
 
         for m in range(micro):
+            left(FWD, m, fwd_straight[m])
+            left(BWD, m, bwd_straight[m])
             sent(HOME, BWD, m, own_bwd[m])
             sent(AWAY, BWD, m, their_bwd[m])
             if own_fwd[m]:
@@ -595,12 +684,7 @@
                 relay_sent(BWD, m)
 
     for m in range(micro):
-        for kind in (FWD, BWD):
-            back_sent(kind, m)
-            for c in range(SPLIT):
-                away_copy(kind, m, c).wait_send()
         section_copy(m).wait_send()
-        sum_copy(m).wait_send()
     route_copy.wait_send()
 
 
@@ -633,13 +717,13 @@
     routes = pltpu.VMEM((8, tok), F32)
     table = pltpu.VMEM((micro, total, tok), BF16)
     out, grad_in, grad_out = pl.pallas_call(
-        functools.partial(kernel, experts, cap, pad, RELAYED),
+        functools.partial(kernel, experts, cap, pad, RELAYED, DIRECT),
         out_shape=(
             pltpu.VMEM((micro, tok, half), BF16),
             pltpu.VMEM((full, hidden_half), BF16),
             pltpu.VMEM((hidden_half, full), BF16),
         ),
-        in_specs=[vmem] * 5 + [anywhere] * 2,
+        in_specs=[anywhere] * 7,
         out_specs=(vmem, vmem, vmem),
         scratch_shapes=[
             table,
@@ -663,12 +747,17 @@
             routes,
             pltpu.VMEM((full, hidden_half), BF16),
             pltpu.VMEM((hidden_half, full), BF16),
-            pltpu.SemaphoreType.DMA((2,)),
+            tokens,
+            pltpu.VMEM((1, full), F32),
+            pltpu.VMEM((micro, tok), F32),
+            pltpu.VMEM((micro, tok), jnp.int32),
+            pltpu.VMEM((micro, tok), jnp.int32),
+            pltpu.SemaphoreType.DMA((7,)),
             pltpu.SemaphoreType.REGULAR,
             per_pair, per_block,
-            per_pair, per_block,
+            per_pair, per_pair,
             per_piece, per_piece,
-            per_pair, per_block,
+            per_pair, per_pair,
             per_micro, per_micro,
             per_micro, per_micro,
             per_pair,

time: 79.2 us -> 73.2 us (0.924)
  Pallas kernels: 78.3 us -> 72.2 us
    pallas_call x1, Pallas kernels: 76 us -> 70 us  [on_device(): pl.pallas_call(functools.partial(kernel, experts, cap, pad, RELAYED, DIRE...]
where the time goes in v3:
time: 73.2 us; the launch traced here: 73 us
  Pallas kernels  72.2 us (99%)
  between operations  0.8 us (1%)
    pallas_call x1, Pallas kernels, on_device(): pl.pallas_call(functools.partial(kernel, experts, cap, pad, RELAYED, DIRE...  70 us
    pallas_call x1, Pallas kernels, on_device(): pl.pallas_call(copy_out, out_shape=[jax.ShapeDtypeStruct(x.shape, x.dtype...  2.26 us

profile of v3, /device:TPU:0, one launch (start us, length us, event | category | flops | bytes accessed | tf_op | source)
XLA Modules:
  0.0 73.0 jit_solution(10654808692216812985)
XLA Ops:
  0.6 70.0 %shard_map.94 = (bf16[2,128,384]{2,1,0:T(8,128)(2,1)S(1)}, bf16[768,1536]{1,0:T(8,128)(2,1)S(1)}, bf16[1536,768]{1,0:T(8,128)(2,1)S(1)}) custom-call(bf16[2,128,384]{2,1,0:T(8,128)(2,1)} %bitcast.11, f32[1,768]{1,0:T(1,128)} %gain_hbm.1, f32[2,128]{1,0:T(2,128)} %bitcast.12, s32[2,128]{1,0:T(2,128)} %bitcast.13, s32[2,128]{1,0:T(2,128)} %bitcast.14, ...), custom_call_target="tpu_custom_call" | custom-call | tf_op jit(solution)/shard_map/pallas_call | solution.py:719
  70.6 2.3 %shard_map.95 = (bf16[2,128,384]{2,1,0:T(8,128)(2,1)}, bf16[768,1536]{1,0:T(8,128)(2,1)}, bf16[1536,768]{1,0:T(8,128)(2,1)}) custom-call(bf16[2,128,384]{2,1,0:T(8,128)(2,1)S(1)} %get-tuple-element.9.out_in, bf16[768,1536]{1,0:T(8,128)(2,1)S(1)} %get-tuple-element.10.gin_in, bf16[1536,768]{1,0:T(8,128)(2,1)S(1)} %get-tuple-element.11.gout_in), custom_call_target="tpu_custom_call" | custom-call | tf_op jit(solution)/shard_map/pallas_call | solution.py:775

commit v4 on v3

--- a/solution.py
+++ b/solution.py
@@ -23,7 +23,8 @@
 RELAY_NEAR = True
 TURN_AT = 0
 HOLD = 1
-TAIL = 0
+TAIL = 7
+PARTS = (1, 1, 1)
 ORDER = 3
 UNROLL = 6
 PUMP_AT = 0
@@ -646,22 +647,39 @@
         if ORDER == 2:
             finish(0)
         grad_partial(1, bwd_straight[1])
+        if TAIL == 5 or TAIL == 6:
+            out_partial(0, fwd_straight[0])
+            out_partial(1, fwd_straight[1])
+        if TAIL == 7:
+            out_partial(0, fwd_straight[0])
         if ORDER == 3:
             finish(0)
         if not bwd_straight[1]:
             send_back(BWD, 1)
+        if TAIL == 7:
+            out_partial(1, fwd_straight[1])
+        if TAIL == 6:
+            in_grads()
         if TAIL == 0:
             out_partial(0, fwd_straight[0])
             out_partial(1, fwd_straight[1])
+        if TAIL == 8:
+            out_partial(0, fwd_straight[0])
         finish(1)
+        if TAIL == 8:
+            in_grads()
+            out_grads()
+            out_partial(1, fwd_straight[1])
         if TAIL == 1:
             out_partial(0, fwd_straight[0])
             out_partial(1, fwd_straight[1])
-        in_grads()
+        if TAIL != 6 and TAIL != 8:
+            in_grads()
         if TAIL == 2:
             out_partial(0, fwd_straight[0])
             out_partial(1, fwd_straight[1])
-        out_grads()
+        if TAIL != 8:
+            out_grads()
         if TAIL == 3:
             out_partial(0, fwd_straight[0])
             out_partial(1, fwd_straight[1])
@@ -690,7 +708,12 @@
 
 def copy_out(out_in, gin_in, gout_in, out_ref, gin_ref, gout_ref, sem):
     pairs = ((gin_in, gin_ref), (gout_in, gout_ref), (out_in, out_ref))
-    copies = [pltpu.make_async_copy(a, b, sem.at[i]) for i, (a, b) in enumerate(pairs)]
+    copies = []
+    for i, (a, b) in enumerate(pairs):
+        step = a.shape[0] // PARTS[i]
+        for j in range(PARTS[i]):
+            part = slice(j * step, (j + 1) * step)
+            copies.append(pltpu.make_async_copy(a.at[part], b.at[part], sem.at[len(copies)]))
     for copy in copies:
         copy.start()
     for copy in copies:
@@ -777,7 +800,7 @@
         out_shape=[jax.ShapeDtypeStruct(x.shape, x.dtype) for x in results],
         in_specs=[vmem] * 3,
         out_specs=[anywhere] * 3,
-        scratch_shapes=[pltpu.SemaphoreType.DMA((3,))],
+        scratch_shapes=[pltpu.SemaphoreType.DMA((sum(PARTS),))],
         compiler_params=pltpu.CompilerParams(vmem_limit_bytes=COPY_LIMIT),
     )(*results)
     return (out[None], grad_in[None, None], grad_out[None, None])

time: 73.2 us -> 72.2 us (0.986)
  Pallas kernels: 72.2 us -> 71.3 us
    pallas_call x1, Pallas kernels: 70 us -> 69 us  [on_device(): pl.pallas_call(functools.partial(kernel, experts, cap, pad, RELAYED, DIRE...]
where the time goes in v4:
time: 72.2 us; the launch traced here: 72.1 us
  Pallas kernels  71.3 us (99%)
  between operations  0.8 us (1%)
    pallas_call x1, Pallas kernels, on_device(): pl.pallas_call(functools.partial(kernel, experts, cap, pad, RELAYED, DIRE...  69 us
    pallas_call x1, Pallas kernels, on_device(): pl.pallas_call(copy_out, out_shape=[jax.ShapeDtypeStruct(x.shape, x.dtype...  2.26 us

profile of v4, /device:TPU:0, one launch (start us, length us, event | category | flops | bytes accessed | tf_op | source)
XLA Modules:
  0.0 72.1 jit_solution(1970290053162051368)
XLA Ops:
  0.6 69.0 %shard_map.94 = (bf16[2,128,384]{2,1,0:T(8,128)(2,1)S(1)}, bf16[768,1536]{1,0:T(8,128)(2,1)S(1)}, bf16[1536,768]{1,0:T(8,128)(2,1)S(1)}) custom-call(bf16[2,128,384]{2,1,0:T(8,128)(2,1)} %bitcast.11, f32[1,768]{1,0:T(1,128)} %gain_hbm.1, f32[2,128]{1,0:T(2,128)} %bitcast.12, s32[2,128]{1,0:T(2,128)} %bitcast.13, s32[2,128]{1,0:T(2,128)} %bitcast.14, ...), custom_call_target="tpu_custom_call" | custom-call | tf_op jit(solution)/shard_map/pallas_call | solution.py:742
  69.7 2.3 %shard_map.95 = (bf16[2,128,384]{2,1,0:T(8,128)(2,1)}, bf16[768,1536]{1,0:T(8,128)(2,1)}, bf16[1536,768]{1,0:T(8,128)(2,1)}) custom-call(bf16[2,128,384]{2,1,0:T(8,128)(2,1)S(1)} %get-tuple-element.9.out_in, bf16[768,1536]{1,0:T(8,128)(2,1)S(1)} %get-tuple-element.10.gin_in, bf16[1536,768]{1,0:T(8,128)(2,1)S(1)} %get-tuple-element.11.gout_in), custom_call_target="tpu_custom_call" | custom-call | tf_op jit(solution)/shard_map/pallas_call | solution.py:798

commit v5 on v4

--- a/solution.py
+++ b/solution.py
@@ -24,7 +24,7 @@
 TURN_AT = 0
 HOLD = 1
 TAIL = 7
-PARTS = (1, 1, 1)
+PARTS = (4, 4, 1)
 ORDER = 3
 UNROLL = 6
 PUMP_AT = 0
@@ -568,9 +568,9 @@
         out_grads()
         if not bwd_straight[1]:
             send_back(BWD, 1)
+        in_grads()
         section_copy(0).wait_recv()
         out_ref[0] = layer_grad(0, sec_in[0], bwd_straight[0])
-        in_grads()
         section_copy(1).wait_recv()
         out_ref[1] = layer_grad(1, sec_in[1], bwd_straight[1])
 

time: 72.2 us -> 72.3 us (level)
  no operation moved by 1% of the time
where the time goes in v5:
time: 72.3 us; the launch traced here: 72.1 us
  Pallas kernels  71.3 us (99%)
  between operations  0.8 us (1%)
    pallas_call x1, Pallas kernels, on_device(): pl.pallas_call(functools.partial(kernel, experts, cap, pad, RELAYED, DIRE...  69 us
    pallas_call x1, Pallas kernels, on_device(): pl.pallas_call(copy_out, out_shape=[jax.ShapeDtypeStruct(x.shape, x.dtype...  2.31 us

profile of v5, /device:TPU:0, one launch (start us, length us, event | category | flops | bytes accessed | tf_op | source)
XLA Modules:
  0.0 72.1 jit_solution(16774618893915717297)
XLA Ops:
  0.6 69.0 %shard_map.94 = (bf16[2,128,384]{2,1,0:T(8,128)(2,1)S(1)}, bf16[768,1536]{1,0:T(8,128)(2,1)S(1)}, bf16[1536,768]{1,0:T(8,128)(2,1)S(1)}) custom-call(bf16[2,128,384]{2,1,0:T(8,128)(2,1)} %bitcast.11, f32[1,768]{1,0:T(1,128)} %gain_hbm.1, f32[2,128]{1,0:T(2,128)} %bitcast.12, s32[2,128]{1,0:T(2,128)} %bitcast.13, s32[2,128]{1,0:T(2,128)} %bitcast.14, ...), custom_call_target="tpu_custom_call" | custom-call | tf_op jit(solution)/shard_map/pallas_call | solution.py:742
  69.7 2.3 %shard_map.95 = (bf16[2,128,384]{2,1,0:T(8,128)(2,1)}, bf16[768,1536]{1,0:T(8,128)(2,1)}, bf16[1536,768]{1,0:T(8,128)(2,1)}) custom-call(bf16[2,128,384]{2,1,0:T(8,128)(2,1)S(1)} %get-tuple-element.9.out_in, bf16[768,1536]{1,0:T(8,128)(2,1)S(1)} %get-tuple-element.10.gin_in, bf16[1536,768]{1,0:T(8,128)(2,1)S(1)} %get-tuple-element.11.gout_in), custom_call_target="tpu_custom_call" | custom-call | tf_op jit(solution)/shard_map/pallas_call | solution.py:798
